TPU v7x, 256 devices: a whole 4x4x8 slice. The times are simulated.
256 devices in a mesh: rows: 32 (over z, x), cols: 8 (over y, core).
Axes of the slice: x: 4, y: 4, z: 8, core: 2. Of those that a mesh axis runs over, the one named last changes fastest.
Arguments:
- features: bfloat16 [524288, 440], P(('rows', 'cols')), may hold values from -12 to 12
- residual: float32 [524288, 147], P(('rows', 'cols')), may hold values from -6 to 6
- coeffs: float32 [524288, 147], P(('rows', 'cols')), may hold values from -3 to 3
- block_inverse: float32 [2, 2048, 2048], P(None, ('rows', 'cols')), may hold values from -0.0234375 to 0.0234375
- block_index: int32 [2, 2048], P(None, 'cols'), may hold values from 0 to 2047, as said below
- owners: int32 [2], replicated, may hold values from 0 to 31
Outputs:
- new_coeffs: float32 [524288, 147], P(('rows', 'cols'))
- new_residual: float32 [524288, 147], P(('rows', 'cols'))
Inputs may be any that keep to these rules, and one draw needn't show every extreme that they name: `block_index`: for each step and each aligned run of 256 positions, the indices are distinct.
All inputs are finite; a program needn't handle non-finite values.
Results may differ from a plain program's by a relative error of at most 0.0028.
Values may be sent and summed in bfloat16 or wider, within the bound.
A program may use at most 64 MiB of HBM per device.

v0:
```python
import jax
import jax.numpy as jnp
from jax import lax
from jax.sharding import Mesh
from jax.sharding import PartitionSpec as P

ROWS = ("rows_0", "rows_1")
COLS = ("cols_0", "cols_1")
ROWS_COLS = ("rows_0", "rows_1", "cols_0", "cols_1")
penalty = 0.5


def from_root(value, axes, root):
    value = jnp.where(lax.axis_index(axes) == root, value, jnp.zeros_like(value))
    for axis in axes:
        value = lax.psum(value, axis)
    return value


def in_order(parts, dim):
    shape = list(parts.shape[1:])
    shape[dim] *= parts.shape[0]
    return jnp.moveaxis(parts, 0, dim).reshape(shape)


def copy_for_each(value, axis):
    copies = jnp.broadcast_to(value, (lax.axis_size(axis), *value.shape))
    return lax.all_to_all(copies, axis, split_axis=0, concat_axis=0, tiled=True)


def collect(value, axis, dim):
    return in_order(copy_for_each(value, axis), dim)


def from_root_2(value, axis, root):
    return lax.dynamic_index_in_dim(lax.all_gather(value, axis), root, 0, keepdims=False)


def stacked_from(value, axes, order):
    parts = value[None]
    for k in order:
        parts = lax.all_gather(parts, axes[k], axis=0, tiled=True)
    block = [lax.axis_size(axes[k]) for k in reversed(order)]
    parts = parts.reshape(*block, *value.shape)
    turned = sorted(range(len(order)), key=lambda place: order[len(order) - 1 - place])
    return parts.transpose(*turned, *range(len(order), parts.ndim)).reshape(-1, *value.shape)


def gather_axes(value, axes, order, dim):
    return in_order(stacked_from(value, axes, order), dim)


def per_device(features, residual, coeffs, block_inverse, block_index, owners):
    frame_count = features.shape[0]
    feature_width = features.shape[1]
    per_col = block_index.shape[1]
    row_block = min(512, frame_count)
    exponent = -1.0 / feature_width
    my_row = lax.axis_index(ROWS)
    my_col = lax.axis_index(COLS)
    squares = jnp.sum(jnp.square(features.astype(jnp.float32)), axis=1)
    feature_blocks = features.reshape(frame_count // row_block, row_block, feature_width)
    norm_blocks = squares.reshape(frame_count // row_block, row_block)
    for step_id in range(block_index.shape[0]):
        chosen_rows = block_index[step_id]
        owner_row = owners[step_id]
        mine_feat = jnp.take(features, chosen_rows, axis=0)
        mine_res = jnp.take(residual, chosen_rows, axis=0)
        row_piece = from_root(mine_feat, ROWS, owner_row)
        chosen = collect(row_piece, COLS, 0)
        res_piece = from_root_2(mine_res, ROWS, owner_row)
        picked_res = collect(res_piece, COLS, 0)
        my_update = jnp.dot(
            block_inverse[step_id],
            picked_res,
            precision=lax.Precision.HIGHEST,
            preferred_element_type=jnp.float32,
        ).astype(jnp.bfloat16)
        update = gather_axes(my_update, ROWS_COLS, (1, 0, 2, 3), 0)
        chosen_norms = jnp.sum(jnp.square(chosen.astype(jnp.float32)), axis=1)

        def kernel_rows(operands):
            block_rows, block_norms = operands
            inner = lax.dot_general(
                block_rows, chosen, (((1,), (1,)), ((), ())), preferred_element_type=jnp.float32
            )
            distance = block_norms[:, None] + chosen_norms[None, :] - 2.0 * inner
            kernel = jnp.exp(distance * exponent).astype(jnp.bfloat16)
            return jnp.dot(kernel, update, preferred_element_type=jnp.float32)

        change = lax.map(kernel_rows, (feature_blocks, norm_blocks)).reshape(frame_count, -1)
        residual = residual - change
        is_owner = jnp.where(my_row == owner_row, 1.0, 0.0).astype(jnp.float32)
        mine_update = (
            lax.dynamic_slice_in_dim(update, my_col * per_col, per_col, 0).astype(jnp.float32)
            * is_owner
        )
        residual = residual.at[chosen_rows].add(-penalty * mine_update)
        coeffs = coeffs.at[chosen_rows].add(mine_update)
    return (coeffs, residual)


def solution(mesh):
    split = Mesh(mesh.devices.reshape(8, 4, 4, 2), ("rows_0", "rows_1", "cols_0", "cols_1"))
    in_specs = (
        P(ROWS_COLS, None),
        P(ROWS_COLS, None),
        P(ROWS_COLS, None),
        P(None, ROWS_COLS, None),
        P(None, COLS),
        P(),
    )
    out_specs = (P(ROWS_COLS, None), P(ROWS_COLS, None))
    return jax.shard_map(
        per_device, mesh=split, in_specs=in_specs, out_specs=out_specs, check_vma=False
    )
```

profile of v0, /device:TPU:1, one launch (start us, length us, event | category | flops | bytes accessed | tf_op | source)
XLA Modules:
  0.0 525.2 jit_solution(5898855721030536369)
XLA Ops:
  21.6 72.7 %all-reduce.5.cloned.1.call-done = (bf16[256,440]{1,0:T(8,128)(2,1)}, bf16[256,440]{1,0:T(8,128)(2,1)}) async-done(((bf16[256,440]{1,0:T(8,128)(2,1)}, bf16[256,440]{1,0:T(8,128)(2,1)}), (bf16[256,440]{1,0:T(8,128)(2,1)}, bf16[256,440]{1,0:T(8,128)(2,1)})) %all-reduce.5.cloned.1.call-update) | async-done | bytes 450576 | tf_op jit(solution)/shard_map/psum | solution.py:16
  97.1 49.7 %all-reduce.7.cloned.1.call-done = (bf16[256,440]{1,0:T(8,128)(2,1)}, bf16[256,440]{1,0:T(8,128)(2,1)}) async-done(((bf16[256,440]{1,0:T(8,128)(2,1)}, bf16[256,440]{1,0:T(8,128)(2,1)}), (bf16[256,440]{1,0:T(8,128)(2,1)}, bf16[256,440]{1,0:T(8,128)(2,1)})) %all-reduce.7.cloned.1.call-update) | async-done | bytes 450576 | tf_op jit(solution)/shard_map/psum | solution.py:16
  149.2 7.2 %all-to-all-start.1 = ((bf16[8,256,440]{1,2,0:T(8,128)(2,1)}), bf16[8,256,440]{1,2,0:T(8,128)(2,1)S(1)}, u32[]{:S(2)}, u32[]{:S(2)}) async-start(bf16[8,256,440]{1,2,0:T(8,128)(2,1)} %broadcast_in_dim.53), calls=%async_computation.1 | async-start | bytes 3604480 | tf_op jit(solution)/shard_map/all_to_all | solution.py:28
  158.1 40.6 %all-gather.7.cloned.1.call-done = f32[8192,147]{1,0:T(8,128)} async-done(((f32[256,147]{1,0:T(8,128)}), f32[8192,147]{1,0:T(8,128)}) %all-gather.7.cloned.1.call-update) | async-done | bytes 4816912 | tf_op jit(solution)/shard_map/all_gather | solution.py:36
  200.9 5.9 %all-to-all-start = ((f32[8,256,147]{1,2,0:T(8,128)}), f32[8,256,147]{1,2,0:T(8,128)S(1)}, u32[]{:S(2)}, u32[]{:S(2)}) async-start(f32[8,256,147]{1,2,0:T(8,128)} %broadcast_in_dim.51), calls=%async_computation | async-start | bytes 2490368 | tf_op jit(solution)/shard_map/all_to_all | solution.py:28
  211.8 12.0 %all-to-all-done = f32[8,256,147]{1,2,0:T(8,128)S(1)} async-done(((f32[8,256,147]{1,2,0:T(8,128)}), f32[8,256,147]{1,2,0:T(8,128)S(1)}, u32[]{:S(2)}, u32[]{:S(2)}) %all-to-all-start) | async-done | bytes 1204256 | tf_op jit(solution)/shard_map/all_to_all | solution.py:28
  226.2 9.1 %all-gather.1 = bf16[32,147]{1,0:T(8,128)(2,1)S(1)} all-gather(bf16[8,147]{1,0:T(8,128)(2,1)S(1)} %fusion.18), channel_id=3, replica_groups=mesh['rows_0'=8,'rows_1'=4,'cols_0'=4,'cols_1'=2] {'rows_1'}, dimensions={0}, use_global_device_ids=true | all-gather | bytes 11760 | tf_op jit(solution)/shard_map/all_gather | solution.py:42
  235.3 18.3 %all_gather.39 = bf16[32,8,147]{2,1,0:T(8,128)(2,1)S(1)} all-gather(bf16[4,8,147]{2,1,0:T(8,128)(2,1)S(1)} %bitcast.119), channel_id=1, replica_groups=mesh['rows_0'=8,'rows_1'=4,'cols_0'=4,'cols_1'=2] {'rows_0'}, dimensions={0}, use_global_device_ids=true | all-gather | bytes 84672 | tf_op jit(solution)/shard_map/all_gather | solution.py:42
  253.6 9.9 %all_gather.40 = bf16[128,8,147]{2,1,0:T(8,128)(2,1)S(1)} all-gather(bf16[32,8,147]{2,1,0:T(8,128)(2,1)S(1)} %all_gather.39), channel_id=1, replica_groups=mesh['rows_0'=8,'rows_1'=4,'cols_0'=4,'cols_1'=2] {'cols_0'}, dimensions={0}, use_global_device_ids=true | all-gather | bytes 376320 | tf_op jit(solution)/shard_map/all_gather | solution.py:42
  264.0 14.9 %all_gather.41 = bf16[256,8,147]{0,1,2:T(8,128)(2,1)S(1)} all-gather(bf16[128,8,147]{0,1,2:T(8,128)(2,1)S(1)} %copy.49), channel_id=1, replica_groups=mesh['rows_0'=8,'rows_1'=4,'cols_0'=4,'cols_1'=2] {'cols_1'}, dimensions={0}, use_global_device_ids=true | all-gather | bytes 903168 | tf_op jit(solution)/shard_map/all_gather | solution.py:42
  281.9 14.0 %while.20 = (s32[]{:T(128)}, f32[4,512,147]{1,2,0:T(8,128)S(1)}, f32[4,512]{1,0:T(4,128)S(1)}, f32[2048]{0:T(1024)S(1)}, bf16[4,512,440]{2,1,0:T(8,128)(2,1)}, /...) while((s32[]{:T(128)}, f32[4,512,147]{1,2,0:T(8,128)S(1)}, f32[4,512]{1,0:T(4,128)S(1)}, ...), condition=%wide.region_6.9_spmd, body=%wide.region_5.8_spmd.sunk | while | flops 1236271104 | bytes 3996769 | solution.py:91
  306.9 4.6 all-to-all-start.3
  313.6 84.1 %all-gather.9.cloned.1.call-done = f32[8192,147]{1,0:T(8,128)} async-done(((f32[256,147]{1,0:T(8,128)}), f32[8192,147]{1,0:T(8,128)}) %all-gather.9.cloned.1.call-update) | async-done | bytes 4816912 | tf_op jit(solution)/shard_map/all_gather | solution.py:36
  399.9 5.8 %all-to-all-start.2 = ((f32[8,256,147]{1,2,0:T(8,128)}), f32[8,256,147]{1,2,0:T(8,128)S(1)}, u32[]{:S(2)}, u32[]{:S(2)}) async-start(f32[8,256,147]{1,2,0:T(8,128)} %broadcast_in_dim.54), calls=%async_computation.2 | async-start | bytes 2490368 | tf_op jit(solution)/shard_map/all_to_all | solution.py:28
  414.1 5.1 scatter_custom_fusion
  424.7 9.1 %all-gather.3 = bf16[32,147]{1,0:T(8,128)(2,1)S(1)} all-gather(bf16[8,147]{1,0:T(8,128)(2,1)S(1)} %fusion.19), channel_id=5, replica_groups=mesh['rows_0'=8,'rows_1'=4,'cols_0'=4,'cols_1'=2] {'rows_1'}, dimensions={0}, use_global_device_ids=true | all-gather | bytes 11760 | tf_op jit(solution)/shard_map/all_gather | solution.py:42
  433.8 18.3 %all_gather.45 = bf16[32,8,147]{2,1,0:T(8,128)(2,1)S(1)} all-gather(bf16[4,8,147]{2,1,0:T(8,128)(2,1)S(1)} %bitcast.120), channel_id=1, replica_groups=mesh['rows_0'=8,'rows_1'=4,'cols_0'=4,'cols_1'=2] {'rows_0'}, dimensions={0}, use_global_device_ids=true | all-gather | bytes 84672 | tf_op jit(solution)/shard_map/all_gather | solution.py:42
  452.1 9.9 %all_gather.46 = bf16[128,8,147]{2,1,0:T(8,128)(2,1)S(1)} all-gather(bf16[32,8,147]{2,1,0:T(8,128)(2,1)S(1)} %all_gather.45), channel_id=1, replica_groups=mesh['rows_0'=8,'rows_1'=4,'cols_0'=4,'cols_1'=2] {'cols_0'}, dimensions={0}, use_global_device_ids=true | all-gather | bytes 376320 | tf_op jit(solution)/shard_map/all_gather | solution.py:42
  462.5 15.1 %all_gather.47 = bf16[256,8,147]{0,1,2:T(8,128)(2,1)} all-gather(bf16[128,8,147]{0,1,2:T(8,128)(2,1)S(1)} %copy.62), channel_id=1, replica_groups=mesh['rows_0'=8,'rows_1'=4,'cols_0'=4,'cols_1'=2] {'cols_1'}, dimensions={0}, use_global_device_ids=true | all-gather | bytes 903168 | tf_op jit(solution)/shard_map/all_gather | solution.py:42
  480.6 5.1 scatter_custom_fusion.2
  488.4 16.6 %while.21 = (s32[]{:T(128)}, f32[4,512,147]{1,2,0:T(8,128)S(1)}, f32[4,512]{1,0:T(4,128)S(1)}, f32[2048]{0:T(1024)S(1)}, bf16[4,512,440]{2,1,0:T(8,128)(2,1)}, /...) while((s32[]{:T(128)}, f32[4,512,147]{1,2,0:T(8,128)S(1)}, f32[4,512]{1,0:T(4,128)S(1)}, ...), condition=%wide.region_13.16_spmd, body=%wide.region_12.15_spmd.sunk | while | flops 1236271104 | bytes 3996769 | solution.py:91
  492.6 4.1 fusion.63
  500.9 4.1 fusion.63
  510.0 5.1 scatter_custom_fusion.3
  (98 shorter events, 93.7 us)
Async XLA Ops:
  8.0 86.4 %all-reduce.5.cloned.1.call-start = ((), (), s32[]{:S(2)}) async-start(), calls=%async_computation.6 | async-start | bytes 1048576 | tf_op jit(solution)/shard_map/psum | solution.py:16
  14.3 3.7 copy-start.1
  16.2 78.3 %copy-start.3 = (f32[2048,147]{0,1:T(8,128)S(1)}, f32[2048,147]{0,1:T(8,128)}, u32[]{:S(2)}) copy-start(f32[2048,147]{0,1:T(8,128)} %param.15) | copy-start | bytes 3612676
  21.6 125.2 %all-reduce.7.cloned.1.call-start = ((), (), s32[]{:S(2)}) async-start(), calls=%async_computation.7 | async-start | bytes 1048576 | tf_op jit(solution)/shard_map/psum | solution.py:16
  94.4 104.3 %all-gather.7.cloned.1.call-start = ((), (), s32[]{:S(2)}) async-start(), calls=%async_computation.4 | async-start | bytes 8650752 | tf_op jit(solution)/shard_map/all_gather | solution.py:36
  95.3 53.9 %copy-start = (f32[2048,147]{1,0:T(8,128)}, f32[2048,147]{1,0:T(8,128)S(1)}, u32[]{:S(2)}) copy-start(f32[2048,147]{1,0:T(8,128)S(1)} %copy.46) | copy-start | bytes 3612676
  149.2 50.6 %all-to-all-start.1 = ((bf16[8,256,440]{1,2,0:T(8,128)(2,1)}), bf16[8,256,440]{1,2,0:T(8,128)(2,1)S(1)}, u32[]{:S(2)}, u32[]{:S(2)}) async-start(bf16[8,256,440]{1,2,0:T(8,128)(2,1)} %broadcast_in_dim.53), calls=%async_computation.1 | async-start | bytes 3604480 | tf_op jit(solution)/shard_map/all_to_all | solution.py:28
  200.9 7.8 %copy-start.6 = (s32[2,256]{1,0:T(2,128)S(1)}, s32[2,256]{1,0:T(2,128)}, u32[]{:S(2)}) copy-start(s32[2,256]{1,0:T(2,128)} %param.18) | copy-start | bytes 6148
  200.9 23.0 %all-to-all-start = ((f32[8,256,147]{1,2,0:T(8,128)}), f32[8,256,147]{1,2,0:T(8,128)S(1)}, u32[]{:S(2)}, u32[]{:S(2)}) async-start(f32[8,256,147]{1,2,0:T(8,128)} %broadcast_in_dim.51), calls=%async_computation | async-start | bytes 2490368 | tf_op jit(solution)/shard_map/all_to_all | solution.py:28
  206.8 190.9 %all-gather.9.cloned.1.call-start = ((), (), s32[]{:S(2)}) async-start(), calls=%async_computation.5 | async-start | bytes 8650752 | tf_op jit(solution)/shard_map/all_gather | solution.py:36
  224.2 0.9 copy-start.5
  280.0 2.0 copy-start.2
  303.6 1.8 copy-start.4
  306.9 91.8 %all-to-all-start.3 = ((bf16[8,256,440]{1,2,0:T(8,128)(2,1)}), bf16[8,256,440]{1,2,0:T(8,128)(2,1)}, u32[]{:S(2)}, u32[]{:S(2)}) async-start(bf16[8,256,440]{1,2,0:T(8,128)(2,1)} %broadcast_in_dim.56), calls=%async_computation.3 | async-start | bytes 3604480 | tf_op jit(solution)/shard_map/all_to_all | solution.py:28
  399.9 22.8 %all-to-all-start.2 = ((f32[8,256,147]{1,2,0:T(8,128)}), f32[8,256,147]{1,2,0:T(8,128)S(1)}, u32[]{:S(2)}, u32[]{:S(2)}) async-start(f32[8,256,147]{1,2,0:T(8,128)} %broadcast_in_dim.54), calls=%async_computation.2 | async-start | bytes 2490368 | tf_op jit(solution)/shard_map/all_to_all | solution.py:28
Sparse Core Ops, SparseCore 0:
  21.7 72.6 all-reduce.4
  96.8 49.8 all-reduce.6
Sparse Core Ops, SparseCore 1:
  98.0 100.6 all-gather.6
  305.5 92.2 all-gather.8
where the time goes:
time: 527 us; the launch traced here: 525 us
  waiting for transfers between devices  263 us (50%)
  blocking collectives  105 us (20%)
  local copies, waits for them, and re-layouts  47.4 us (9%)
  other arithmetic  33.4 us (6%)
  matrix products  32.5 us (6%)
  starting transfers between devices  23.5 us (4%)
  between operations  20.9 us (4%)
    all_gather x2, waiting for transfers between devices, from_root_2(): lax.all_gather(value, axis)  125 us
    psum x2, waiting for transfers between devices, from_root(): value = lax.psum(value, axis)  122 us
    all_gather x8, blocking collectives, stacked_from(): parts = lax.all_gather(parts, axes[k], axis=0, tiled=True)  105 us
    dot_general x8, matrix products, kernel_rows(): return jnp.dot(kernel, update, preferred_element_type=jnp.float32)  30.4 us
    all_to_all x4, starting transfers between devices, copy_for_each(): return lax.all_to_all(copies, axis, split_axis=0, concat_axis=0, tiled=True)  23.4 us
    all_to_all x4, waiting for transfers between devices, copy_for_each(): return lax.all_to_all(copies, axis, split_axis=0, concat_axis=0, tiled=True)  15.6 us
    unnamed x27, local copies, waits for them, and re-layouts  14.1 us
  transfers between devices with their start and end apart: 8, of which 6 were waited for; matrix products, arithmetic and copies ran while one was open for 5% of the time, Pallas kernels for 0%

commit v1 on v0

--- a/solution.py
+++ b/solution.py
@@ -13,7 +13,8 @@
 def from_root(value, axes, root):
     value = jnp.where(lax.axis_index(axes) == root, value, jnp.zeros_like(value))
     for axis in axes:
-        value = lax.psum(value, axis)
+        pieces = lax.all_gather(value, axis, axis=0, tiled=False)
+        value = pieces.sum(axis=0)
     return value
 
 

time: 527 us -> 487 us (0.924)
  waiting for transfers between devices: 263 us -> 185 us
  blocking collectives: 105 us -> 131 us
  starting transfers between devices: 23.5 us -> 31.6 us
    psum x2 -> x0, waiting for transfers between devices: 122 us -> none  [from_root(): value = lax.psum(value, axis)]
    all_gather x0 -> x2, waiting for transfers between devices: none -> 37.9 us  [from_root(): pieces = lax.all_gather(value, axis, axis=0, tiled=False)]
    all_gather x0 -> x2, blocking collectives: none -> 26 us  [from_root(): pieces = lax.all_gather(value, axis, axis=0, tiled=False)]
    all_gather x2, waiting for transfers between devices: 125 us -> 139 us  [from_root_2(): lax.all_gather(value, axis)]
    all_to_all x4, starting transfers between devices: 23.4 us -> 31.5 us  [copy_for_each(): return lax.all_to_all(copies, axis, split_axis=0, concat_axis=0, tiled=True)]
    all_to_all x4, waiting for transfers between devices: 15.6 us -> 8.72 us  [copy_for_each(): return lax.all_to_all(copies, axis, split_axis=0, concat_axis=0, tiled=True)]
    unnamed x27 -> x31, local copies, waits for them, and re-layouts: 14.1 us -> 12.7 us
  transfers between devices with their start and end apart: 8 -> 8, of which waited for: 6 -> 5; matrix products, arithmetic and copies ran while one was open for 5% -> 14% of each run, Pallas kernels for 0% -> 0%
where the time goes in v1:
time: 487 us; the launch traced here: 486 us
  waiting for transfers between devices  185 us (38%)
  blocking collectives  131 us (27%)
  local copies, waits for them, and re-layouts  46.7 us (10%)
  other arithmetic  37.5 us (8%)
  matrix products  34.4 us (7%)
  starting transfers between devices  31.6 us (6%)
  between operations  19.2 us (4%)
    all_gather x2, waiting for transfers between devices, from_root_2(): lax.all_gather(value, axis)  139 us
    all_gather x8, blocking collectives, stacked_from(): parts = lax.all_gather(parts, axes[k], axis=0, tiled=True)  105 us
    all_gather x2, waiting for transfers between devices, from_root(): pieces = lax.all_gather(value, axis, axis=0, tiled=False)  37.9 us
    dot_general x8, matrix products, kernel_rows(): return jnp.dot(kernel, update, preferred_element_type=jnp.float32)  32.3 us
    all_to_all x4, starting transfers between devices, copy_for_each(): return lax.all_to_all(copies, axis, split_axis=0, concat_axis=0, tiled=True)  31.5 us
    all_gather x2, blocking collectives, from_root(): pieces = lax.all_gather(value, axis, axis=0, tiled=False)  26 us
    unnamed x31, local copies, waits for them, and re-layouts  12.7 us
    while x4, local copies, waits for them, and re-layouts, per_device(): lax.map(kernel_rows, (feature_blocks, norm_blocks)).reshape(frame_count, -1)  11.2 us
  transfers between devices with their start and end apart: 8, of which 5 were waited for; matrix products, arithmetic and copies ran while one was open for 14% of the time, Pallas kernels for 0%

profile of v1, /device:TPU:1, one launch (start us, length us, event | category | flops | bytes accessed | tf_op | source)
XLA Modules:
  0.0 486.1 jit_solution(17419542322727183345)
XLA Ops:
  19.3 37.9 %all-gather.15.cloned.1.call-done = bf16[2048,440]{1,0:T(8,128)(2,1)} async-done(((bf16[256,440]{1,0:T(8,128)(2,1)}), bf16[2048,440]{1,0:T(8,128)(2,1)}) %all-gather.15.cloned.1.call-update) | async-done | bytes 1802256 | tf_op jit(solution)/shard_map/all_gather | solution.py:16
  59.2 12.9 %all-gather.3 = bf16[1024,440]{1,0:T(8,128)(2,1)S(1)} all-gather(bf16[256,440]{1,0:T(8,128)(2,1)S(1)} %reduce_sum.80), channel_id=5, replica_groups=mesh['rows_0'=8,'rows_1'=4,'cols_0'=4,'cols_1'=2] {'rows_1'}, dimensions={0}, use_global_device_ids=true | all-gather | bytes 1126400 | tf_op jit(solution)/shard_map/all_gather | solution.py:16
  73.9 11.7 %all-to-all-start.1 = ((bf16[8,256,440]{1,2,0:T(8,128)(2,1)}), bf16[8,256,440]{1,2,0:T(8,128)(2,1)}, u32[]{:S(2)}, u32[]{:S(2)}) async-start(bf16[8,256,440]{1,2,0:T(8,128)(2,1)} %broadcast_in_dim.53), calls=%async_computation.1 | async-start | bytes 3604480 | tf_op jit(solution)/shard_map/all_to_all | solution.py:29
  87.5 72.9 %all-gather.13.cloned.1.call-done = f32[8192,147]{1,0:T(8,128)} async-done(((f32[256,147]{1,0:T(8,128)}), f32[8192,147]{1,0:T(8,128)}) %all-gather.13.cloned.1.call-update) | async-done | bytes 4816912 | tf_op jit(solution)/shard_map/all_gather | solution.py:37
  162.6 5.7 %all-to-all-start = ((f32[8,256,147]{1,2,0:T(8,128)}), f32[8,256,147]{1,2,0:T(8,128)S(1)}, u32[]{:S(2)}, u32[]{:S(2)}) async-start(f32[8,256,147]{1,2,0:T(8,128)} %broadcast_in_dim.51), calls=%async_computation | async-start | bytes 2490368 | tf_op jit(solution)/shard_map/all_to_all | solution.py:29
  180.2 5.1 %all-to-all-done = f32[8,256,147]{1,2,0:T(8,128)S(1)} async-done(((f32[8,256,147]{1,2,0:T(8,128)}), f32[8,256,147]{1,2,0:T(8,128)S(1)}, u32[]{:S(2)}, u32[]{:S(2)}) %all-to-all-start) | async-done | bytes 1204256 | tf_op jit(solution)/shard_map/all_to_all | solution.py:29
  187.7 9.8 %all-gather.1 = bf16[32,147]{1,0:T(8,128)(2,1)S(1)} all-gather(bf16[8,147]{1,0:T(8,128)(2,1)S(1)} %fusion.18), channel_id=3, replica_groups=mesh['rows_0'=8,'rows_1'=4,'cols_0'=4,'cols_1'=2] {'rows_1'}, dimensions={0}, use_global_device_ids=true | all-gather | bytes 11760 | tf_op jit(solution)/shard_map/all_gather | solution.py:43
  197.5 19.8 %all_gather.63 = bf16[32,8,147]{2,1,0:T(8,128)(2,1)S(1)} all-gather(bf16[4,8,147]{2,1,0:T(8,128)(2,1)S(1)} %bitcast.127), channel_id=1, replica_groups=mesh['rows_0'=8,'rows_1'=4,'cols_0'=4,'cols_1'=2] {'rows_0'}, dimensions={0}, use_global_device_ids=true | all-gather | bytes 84672 | tf_op jit(solution)/shard_map/all_gather | solution.py:43
  217.2 10.2 %all_gather.64 = bf16[128,8,147]{2,1,0:T(8,128)(2,1)S(1)} all-gather(bf16[32,8,147]{2,1,0:T(8,128)(2,1)S(1)} %all_gather.63), channel_id=1, replica_groups=mesh['rows_0'=8,'rows_1'=4,'cols_0'=4,'cols_1'=2] {'cols_0'}, dimensions={0}, use_global_device_ids=true | all-gather | bytes 376320 | tf_op jit(solution)/shard_map/all_gather | solution.py:43
  227.9 12.7 %all_gather.65 = bf16[256,8,147]{0,1,2:T(8,128)(2,1)} all-gather(bf16[128,8,147]{0,1,2:T(8,128)(2,1)S(1)} %copy.121), channel_id=1, replica_groups=mesh['rows_0'=8,'rows_1'=4,'cols_0'=4,'cols_1'=2] {'cols_1'}, dimensions={0}, use_global_device_ids=true | all-gather | bytes 903168 | tf_op jit(solution)/shard_map/all_gather | solution.py:43
  243.8 15.9 %while.20 = (s32[]{:T(128)}, f32[4,512,147]{1,2,0:T(8,128)S(1)}, f32[4,512]{1,0:T(4,128)S(1)}, f32[2048]{0:T(1024)S(1)}, bf16[4,512,440]{2,1,0:T(8,128)(2,1)S(1)...) while((s32[]{:T(128)}, f32[4,512,147]{1,2,0:T(8,128)S(1)}, f32[4,512]{1,0:T(4,128)S(1)}, ...), condition=%wide.region_6.9_spmd, body=%wide.region_5.8_spmd.sunk | while | flops 1236271104 | bytes 3996761 | solution.py:92
  271.2 13.1 %all-gather.7 = bf16[1024,440]{1,0:T(8,128)(2,1)S(1)} all-gather(bf16[256,440]{1,0:T(8,128)(2,1)S(1)} %reduce_sum.84), channel_id=9, replica_groups=mesh['rows_0'=8,'rows_1'=4,'cols_0'=4,'cols_1'=2] {'rows_1'}, dimensions={0}, use_global_device_ids=true | all-gather | bytes 1126400 | tf_op jit(solution)/shard_map/all_gather | solution.py:16
  286.1 8.4 %all-to-all-start.3 = ((bf16[8,256,440]{1,2,0:T(8,128)(2,1)}), bf16[8,256,440]{1,2,0:T(8,128)(2,1)}, u32[]{:S(2)}, u32[]{:S(2)}) async-start(bf16[8,256,440]{1,2,0:T(8,128)(2,1)} %broadcast_in_dim.56), calls=%async_computation.3 | async-start | bytes 3604480 | tf_op jit(solution)/shard_map/all_to_all | solution.py:29
  296.3 65.9 %all-gather.17.cloned.1.call-done = f32[8192,147]{1,0:T(8,128)} async-done(((f32[256,147]{1,0:T(8,128)}), f32[8192,147]{1,0:T(8,128)}) %all-gather.17.cloned.1.call-update) | async-done | bytes 4816912 | tf_op jit(solution)/shard_map/all_gather | solution.py:37
  364.4 5.7 %all-to-all-start.2 = ((f32[8,256,147]{1,2,0:T(8,128)}), f32[8,256,147]{1,2,0:T(8,128)S(1)}, u32[]{:S(2)}, u32[]{:S(2)}) async-start(f32[8,256,147]{1,2,0:T(8,128)} %broadcast_in_dim.54), calls=%async_computation.2 | async-start | bytes 2490368 | tf_op jit(solution)/shard_map/all_to_all | solution.py:29
  378.5 5.0 %scatter_custom_fusion = f32[2048,147]{1,0:T(8,128)} fusion(f32[2048,147]{1,0:T(8,128)} %copy.124, s32[256]{0:T(256)} %bitcast.144, f32[]{:T(128)S(6)} %select_n.70, bf16[2048,147]{1,0:T(8,128)(2,1)} %get-tuple-element.337, s32[]{:T(128)S(6)} %select_n.69, s32[]{:T(128)} %constant.60.clone.1), kind=kCustom, calls=%fused_computation.46 | custom fusion | flops 112896 | bytes 1335816 | tf_op jit(solution)/shard_map/scatter-add | solution.py:100
  389.1 9.1 %all-gather.5 = bf16[32,147]{1,0:T(8,128)(2,1)S(1)} all-gather(bf16[8,147]{1,0:T(8,128)(2,1)S(1)} %fusion.19), channel_id=7, replica_groups=mesh['rows_0'=8,'rows_1'=4,'cols_0'=4,'cols_1'=2] {'rows_1'}, dimensions={0}, use_global_device_ids=true | all-gather | bytes 11760 | tf_op jit(solution)/shard_map/all_gather | solution.py:43
  398.3 18.3 %all_gather.73 = bf16[32,8,147]{2,1,0:T(8,128)(2,1)S(1)} all-gather(bf16[4,8,147]{2,1,0:T(8,128)(2,1)S(1)} %bitcast.128), channel_id=1, replica_groups=mesh['rows_0'=8,'rows_1'=4,'cols_0'=4,'cols_1'=2] {'rows_0'}, dimensions={0}, use_global_device_ids=true | all-gather | bytes 84672 | tf_op jit(solution)/shard_map/all_gather | solution.py:43
  416.6 9.9 %all_gather.74 = bf16[128,8,147]{2,1,0:T(8,128)(2,1)S(1)} all-gather(bf16[32,8,147]{2,1,0:T(8,128)(2,1)S(1)} %all_gather.73), channel_id=1, replica_groups=mesh['rows_0'=8,'rows_1'=4,'cols_0'=4,'cols_1'=2] {'cols_0'}, dimensions={0}, use_global_device_ids=true | all-gather | bytes 376320 | tf_op jit(solution)/shard_map/all_gather | solution.py:43
  426.9 15.3 %all_gather.75 = bf16[256,8,147]{0,1,2:T(8,128)(2,1)} all-gather(bf16[128,8,147]{0,1,2:T(8,128)(2,1)S(1)} %copy.135), channel_id=1, replica_groups=mesh['rows_0'=8,'rows_1'=4,'cols_0'=4,'cols_1'=2] {'cols_1'}, dimensions={0}, use_global_device_ids=true | all-gather | bytes 903168 | tf_op jit(solution)/shard_map/all_gather | solution.py:43
  445.4 16.6 %while.21 = (s32[]{:T(128)}, f32[4,512,147]{1,2,0:T(8,128)S(1)}, f32[4,512]{1,0:T(4,128)S(1)}, f32[2048]{0:T(1024)S(1)}, bf16[4,512,440]{2,1,0:T(8,128)(2,1)}, /...) while((s32[]{:T(128)}, f32[4,512,147]{1,2,0:T(8,128)S(1)}, f32[4,512]{1,0:T(4,128)S(1)}, ...), condition=%wide.region_13.16_spmd, body=%wide.region_12.15_spmd.sunk | while | flops 1236271104 | bytes 3996761 | solution.py:92
  449.5 4.1 fusion.63
  457.8 4.1 fusion.63
  467.0 5.1 %scatter_custom_fusion.3 = f32[2048,147]{1,0:T(8,128)} fusion(f32[2048,147]{1,0:T(8,128)} %bitcast_subtract_fusion, s32[256]{0:T(256)S(1)} %bitcast.141, f32[]{:T(128)S(6)} %select_n.75, f32[]{:T(128)} %constant.94.clone.1, bf16[2048,147]{1,0:T(8,128)(2,1)} %get-tuple-element.338, s32[]{:T(128)S(6)} %select_n.69, s32[]{:T(128)} %constant.60.clone.1), kind=kCustom, calls=%fused_computation.39 | custom fusion | flops 150528 | bytes 1336328 | tf_op jit(solution)/shard_map/scatter-add | solution.py:99
  (106 shorter events, 104.1 us)
Async XLA Ops:
  7.2 50.0 %all-gather.15.cloned.1.call-start = ((), (), s32[]{:S(2)}) async-start(), calls=%async_computation.5 | async-start | bytes 2359296 | tf_op jit(solution)/shard_map/all_gather | solution.py:16
  12.2 4.4 copy-start.1
  12.2 4.5 copy-start.4
  16.6 143.8 %all-gather.13.cloned.1.call-start = ((), (), s32[]{:S(2)}) async-start(), calls=%async_computation.4 | async-start | bytes 8650752 | tf_op jit(solution)/shard_map/all_gather | solution.py:37
  17.4 41.7 %copy-start = (f32[2048,147]{1,0:T(8,128)}, f32[2048,147]{1,0:T(8,128)S(1)}, u32[]{:S(2)}) copy-start(f32[2048,147]{1,0:T(8,128)S(1)} %copy.118) | copy-start | bytes 3612676
  73.9 87.6 %all-to-all-start.1 = ((bf16[8,256,440]{1,2,0:T(8,128)(2,1)}), bf16[8,256,440]{1,2,0:T(8,128)(2,1)}, u32[]{:S(2)}, u32[]{:S(2)}) async-start(bf16[8,256,440]{1,2,0:T(8,128)(2,1)} %broadcast_in_dim.53), calls=%async_computation.1 | async-start | bytes 3604480 | tf_op jit(solution)/shard_map/all_to_all | solution.py:29
  161.3 7.6 %copy-start.2 = (bf16[2048,440]{1,0:T(8,128)(2,1)S(1)}, bf16[2048,440]{1,0:T(8,128)(2,1)}, u32[]{:S(2)}) copy-start(bf16[2048,440]{1,0:T(8,128)(2,1)} %copy-done.1) | copy-start | bytes 5406724
  162.6 22.8 %all-to-all-start = ((f32[8,256,147]{1,2,0:T(8,128)}), f32[8,256,147]{1,2,0:T(8,128)S(1)}, u32[]{:S(2)}, u32[]{:S(2)}) async-start(f32[8,256,147]{1,2,0:T(8,128)} %broadcast_in_dim.51), calls=%async_computation | async-start | bytes 2490368 | tf_op jit(solution)/shard_map/all_to_all | solution.py:29
  168.3 100.9 %all-gather.19.cloned.1.call-start = ((), (), s32[]{:S(2)}) async-start(), calls=%async_computation.7 | async-start | bytes 2359296 | tf_op jit(solution)/shard_map/all_gather | solution.py:16
  168.9 5.6 %copy-start.6 = (s32[2,256]{1,0:T(2,128)S(1)}, s32[2,256]{1,0:T(2,128)}, u32[]{:S(2)}) copy-start(s32[2,256]{1,0:T(2,128)} %param.18) | copy-start | bytes 6148
  172.6 189.6 %all-gather.17.cloned.1.call-start = ((), (), s32[]{:S(2)}) async-start(), calls=%async_computation.6 | async-start | bytes 8650752 | tf_op jit(solution)/shard_map/all_gather | solution.py:37
  174.5 89.5 %copy-start.7 = (s32[256,1]{0,1:T(1,128)}, s32[256,1]{0,1:T(1,128)S(1)}, u32[]{:S(2)}) copy-start(s32[256,1]{0,1:T(1,128)S(1)} %get-tuple-element.181) | copy-start | bytes 3076
  185.7 0.9 copy-start.5
  286.1 77.2 %all-to-all-start.3 = ((bf16[8,256,440]{1,2,0:T(8,128)(2,1)}), bf16[8,256,440]{1,2,0:T(8,128)(2,1)}, u32[]{:S(2)}, u32[]{:S(2)}) async-start(bf16[8,256,440]{1,2,0:T(8,128)(2,1)} %broadcast_in_dim.56), calls=%async_computation.3 | async-start | bytes 3604480 | tf_op jit(solution)/shard_map/all_to_all | solution.py:29
  364.4 22.8 %all-to-all-start.2 = ((f32[8,256,147]{1,2,0:T(8,128)}), f32[8,256,147]{1,2,0:T(8,128)S(1)}, u32[]{:S(2)}, u32[]{:S(2)}) async-start(f32[8,256,147]{1,2,0:T(8,128)} %broadcast_in_dim.54), calls=%async_computation.2 | async-start | bytes 2490368 | tf_op jit(solution)/shard_map/all_to_all | solution.py:29
  472.0 2.8 copy-start.3
Sparse Core Ops, SparseCore 0:
  16.7 40.4 all-gather.14
  60.3 99.9 all-gather.12
  172.7 33.8 all-gather.18
  269.3 92.8 all-gather.16
